TPU v7x, 32 devices: a whole 2x2x4 slice. The times are simulated.
32 devices in a mesh: parts: 2 (over x), ctx: 8 (over z, y), grp: 2 (over core).
Axes of the slice: x: 2, y: 2, z: 4, core: 2. Of those that a mesh axis runs over, the one named last changes fastest.
Arguments:
- hidden_in: bfloat16 [4, 1024, 2048], P(('parts', 'grp'), 'ctx'), parts along dimension 0, may hold values from -6 to 6
- query_in: bfloat16 [4, 1024, 2048], P(('parts', 'grp'), 'ctx'), parts along dimension 0, may hold values from -6 to 6
- key_in: bfloat16 [4, 1024, 256], P(('parts', 'grp'), 'ctx'), parts along dimension 0, may hold values from -6 to 6
- value_in: bfloat16 [4, 1024, 256], P(('parts', 'grp'), 'ctx'), parts along dimension 0, may hold values from -6 to 6
- positions: int32 [3, 4, 1024], P(None, ('parts', 'grp'), 'ctx'), parts along dimension 1, may hold values from 0 to 1023, as said below
- segments: int32 [4, 1024], P(('parts', 'grp'), 'ctx'), parts along dimension 0, may hold values from 0 to 7, never falling along the last dimension, each value on 1 to 512 neighbouring positions
- expert_ids: int32 [4, 1024, 8], P(('parts', 'grp'), 'ctx'), parts along dimension 0, may hold values from 0 to 15, all different within a row; in each aligned block of 128 rows (0 to 127, 128 to 255, ..., all dimensions but the last counted through in order) at most 72 rows name the same one
- w_out: bfloat16 [2048, 2048], P(('ctx', 'grp')), may hold values from -0.125 to 0.125
- w_router: bfloat16 [2048, 16], replicated, may hold values from -0.03125 to 0.03125
- w_gate: bfloat16 [16, 2048, 768], P(('ctx', 'grp')), may hold values from -0.125 to 0.125
- w_up: bfloat16 [16, 2048, 768], P(('ctx', 'grp')), may hold values from -0.125 to 0.125
- w_down: bfloat16 [16, 768, 2048], P(('ctx', 'grp')), may hold values from -0.21875 to 0.21875
Outputs:
- residual: bfloat16 [4, 1024, 2048], P(('parts', 'grp'), 'ctx'), parts along dimension 0
- layer_out: bfloat16 [4, 1024, 2048], P(('parts', 'grp'), 'ctx'), parts along dimension 0
There are 2 independent parts, one for each index of `parts`. A program takes and returns all parts, laid end to end along the dimension named above; an argument that names none is the same for every part. Nothing has to cross between parts.
Inputs may be any that keep to these rules, and one draw needn't show every extreme that they name: `positions`: t never falls along a sequence; a text token has time, row and column equal; the tokens of an image share one time and cover a grid of rows and columns. `segments`: ids never fall along a sequence; a document has at most 512 tokens and one has exactly that many. `expert_ids`: the 8 experts of a token differ; among the tokens of one device no expert is chosen more than 72 times, and on some device one expert is chosen exactly 72 times.
All inputs are finite; a program needn't handle non-finite values.
Results may differ from a plain program's by a relative error of at most 0.0055.
Values may be sent and summed in bfloat16 or wider, within the bound.
A program may use at most 192 MiB of HBM per device.

v0:
```python
import math

import jax
import jax.numpy as jnp
import numpy as np
from jax import lax
from jax.sharding import PartitionSpec as P

D = 2048
HEADS = 16
KV_HEADS = 2
HD = 128
TOP = 8


rope_base = 5000000.0
norm_eps = 1e-06


def row_norm(values):
    return values * lax.rsqrt(jnp.mean(values * values, axis=-1, keepdims=True) + norm_eps)


def rope_angles(places):
    half_size = HD // 2
    freq_index = jnp.arange(half_size, dtype=jnp.int32)
    inverse = jnp.exp(freq_index.astype(jnp.float32) * (-2.0 * math.log(rope_base) / HD))
    freq_table = np.arange(half_size)
    component = np.where(freq_table < half_size - 4, freq_table % 3, 0)
    picked = places[component, :]
    return jnp.transpose(picked).astype(jnp.float32) * inverse[None, :]


def rotate(head_rows, angles):
    half_size = HD // 2
    cosine = jnp.cos(angles)[:, None, :]
    sine_part = jnp.sin(angles)[:, None, :]
    first_half = head_rows[..., :half_size]
    second_half = head_rows[..., half_size:]
    return jnp.concatenate(
        [
            first_half * cosine - second_half * sine_part,
            second_half * cosine + first_half * sine_part,
        ],
        axis=-1,
    )


def prepare(raw_rows, head_count, angles):
    length = raw_rows.shape[0]
    head_rows = raw_rows.astype(jnp.float32).reshape(length, head_count, HD)
    return rotate(row_norm(head_rows), angles).astype(jnp.bfloat16).reshape(length, head_count * HD)


def to_kv_major(query_rows):
    row_count = query_rows.shape[0]
    group_size = HEADS // KV_HEADS
    arranged = query_rows.reshape(row_count, KV_HEADS, group_size, HD).transpose(1, 2, 0, 3)
    return arranged.reshape(KV_HEADS, group_size * row_count, HD)


def from_kv_major(head_major, row_count):
    group_size = HEADS // KV_HEADS
    arranged = head_major.reshape(KV_HEADS, group_size, row_count, HD).transpose(2, 0, 1, 3)
    return arranged.reshape(row_count, HEADS * HD)


def attend_update(query_mat, query_pos, query_seg, key_piece):
    key_rows, value_rows, key_seg = key_piece
    key_count = key_rows.shape[0]
    group_size = HEADS // KV_HEADS
    key_heads = key_rows.reshape(key_count, KV_HEADS, HD)
    value_heads = value_rows.reshape(key_count, KV_HEADS, HD)
    scores = jnp.einsum(
        "hrd,khd->hrk", query_mat, key_heads, preferred_element_type=jnp.float32
    ) * (1.0 / math.sqrt(HD))
    key_pos = jnp.arange(key_count, dtype=jnp.int32)
    allowed = (key_pos[None, :] <= query_pos[:, None]) & (key_seg[None, :] == query_seg[:, None])
    allowed = jnp.tile(allowed, (group_size, 1))
    weights = jnp.where(allowed[None], jnp.exp(scores), 0.0)
    weighted = jnp.einsum(
        "hrk,khd->hrd",
        weights.astype(jnp.bfloat16),
        value_heads,
        preferred_element_type=jnp.float32,
    )
    totals = jnp.sum(weights, axis=-1)
    return (weighted, totals)


def route_gates(logits, flat_ids):
    matches = flat_ids[:, :, None] == jnp.arange(logits.shape[1], dtype=jnp.int32)[None, None, :]
    picked = jnp.sum(jnp.where(matches, logits[:, None, :], 0.0), axis=-1)
    raised = jnp.exp(picked)
    return raised / jnp.sum(raised, axis=-1, keepdims=True)


def expert_mlp(rows_in, gate_mat, up_mat, down_mat):
    gate_part = jnp.dot(rows_in, gate_mat, preferred_element_type=jnp.float32)
    up_part = jnp.dot(rows_in, up_mat, preferred_element_type=jnp.float32)
    acts = (jax.nn.silu(gate_part) * up_part).astype(jnp.bfloat16)
    return jnp.dot(acts, down_mat, preferred_element_type=jnp.float32).astype(jnp.bfloat16)


def on_device(
    hidden_in,
    query_in,
    key_in,
    value_in,
    positions,
    segments,
    expert_ids,
    w_out,
    w_router,
    w_gate,
    w_up,
    w_down,
):
    tokens = hidden_in.shape[1]
    ctx_place = lax.axis_index("ctx")
    group_size = HEADS // KV_HEADS
    angles = rope_angles(positions[:, 0, :])
    query_rot = prepare(query_in[0], HEADS, angles)
    key_rot = prepare(key_in[0], KV_HEADS, angles)
    own_seg = segments[0]
    first_pos = ctx_place * tokens
    query_blocks = [
        (to_kv_major(query_rot), first_pos + jnp.arange(tokens, dtype=jnp.int32), own_seg)
    ]
    initial = tuple(
        (
            (
                jnp.zeros((KV_HEADS, group_size * block_data[1].shape[0], HD), jnp.float32),
                jnp.zeros((KV_HEADS, group_size * block_data[1].shape[0]), jnp.float32),
            )
            for block_data in query_blocks
        )
    )
    key_piece = (
        lax.all_gather(key_rot, "ctx", axis=0, tiled=True),
        lax.all_gather(value_in[0], "ctx", axis=0, tiled=True),
        lax.all_gather(own_seg, "ctx", axis=0, tiled=True),
    )
    first_key = jnp.int32(0)
    updated = []
    for fold_block_data, state_pair in zip(query_blocks, initial):
        query_mat, query_pos, query_seg = fold_block_data
        updated.append(
            lax.cond(
                first_key <= query_pos[-1],
                lambda held_state, qmat=query_mat, qpos=query_pos, qseg=query_seg: attend_update(
                    qmat, qpos, qseg, key_piece
                ),
                lambda held_state: held_state,
                state_pair,
            )
        )
    folded = tuple(updated)
    results = [
        from_kv_major(weighted / totals[..., None], block_data[1].shape[0]).astype(jnp.bfloat16)
        for block_data, (weighted, totals) in zip(query_blocks, folded)
    ]
    attention = results[0]
    projected = jnp.dot(
        attention,
        lax.all_gather(w_out, ("ctx", "grp"), axis=0, tiled=True),
        preferred_element_type=jnp.float32,
    )
    residual = (hidden_in[0].astype(jnp.float32) + projected).astype(jnp.bfloat16)
    normed = row_norm(residual.astype(jnp.float32)).astype(jnp.bfloat16)
    logits = jnp.dot(normed, w_router, preferred_element_type=jnp.float32)
    own_ids = expert_ids[0]
    gates = route_gates(logits, own_ids)
    expert_count = w_router.shape[1]
    capacity = 9 * tokens * TOP // (8 * expert_count)
    flat_ids = own_ids.reshape(-1)
    matches = (flat_ids[:, None] == jnp.arange(expert_count, dtype=jnp.int32)[None, :]).astype(
        jnp.int32
    )
    running_count = jnp.cumsum(matches, axis=0)
    slot_rank = jnp.sum(matches * (running_count - 1), axis=1)
    slot_place = flat_ids * capacity + slot_rank
    send_rows = (
        jnp.zeros((expert_count * capacity, D), jnp.bfloat16)
        .at[slot_place]
        .set(jnp.repeat(normed, TOP, axis=0))
    )
    received = lax.all_to_all(
        send_rows.reshape(expert_count, capacity, D),
        ("ctx", "grp"),
        split_axis=0,
        concat_axis=0,
        tiled=True,
    )
    produced = expert_mlp(received.reshape(-1, D), w_gate[0], w_up[0], w_down[0])
    answered = lax.all_to_all(
        produced.reshape(received.shape), ("ctx", "grp"), split_axis=0, concat_axis=0, tiled=True
    )
    fetched = answered.reshape(expert_count * capacity, D)[slot_place].reshape(tokens, TOP, D)
    mixture = jnp.einsum("tk,tkd->td", gates, fetched, preferred_element_type=jnp.float32)
    layer_out = (residual.astype(jnp.float32) + mixture).astype(jnp.bfloat16)
    return (residual[None], layer_out[None])


def solution(mesh):
    placed = (
        P(("parts", "grp"), "ctx", None),
        P(("parts", "grp"), "ctx", None),
        P(("parts", "grp"), "ctx", None),
        P(("parts", "grp"), "ctx", None),
        P(None, ("parts", "grp"), "ctx"),
        P(("parts", "grp"), "ctx"),
        P(("parts", "grp"), "ctx", None),
        P(("ctx", "grp"), None),
        P(),
        P(("ctx", "grp"), None, None),
        P(("ctx", "grp"), None, None),
        P(("ctx", "grp"), None, None),
    )
    return jax.shard_map(
        on_device,
        mesh=mesh,
        in_specs=placed,
        out_specs=(P(("parts", "grp"), "ctx", None), P(("parts", "grp"), "ctx", None)),
        check_vma=False,
    )
```

profile of v0, /device:TPU:15, one launch (start us, length us, event | category | flops | bytes accessed | tf_op | source)
XLA Modules:
  0.0 393.7 jit_solution(7726072849400682051)
XLA Ops:
  9.0 1.1 convert_bitcast_fusion
  13.1 1.6 broadcast_multiply_fusion
  19.3 11.6 %all-gather = s32[1,1024]{1,0:T(1,128)S(1)} all-gather(s32[1,128]{1,0:T(1,128)S(1)} %copy-done.7), channel_id=2, replica_groups=mesh['parts'=2,'ctx'=8,'grp'=2] {'ctx'}, dimensions={1}, use_global_device_ids=true | all-gather | bytes 4608 | tf_op jit(solution)/shard_map/all_gather | solution.py:142
  30.8 1.5 maximum_bitcast_fusion
  32.3 29.1 %all_gather.13 = bf16[1024,256]{1,0:T(8,128)(2,1)S(1)} all-gather(bf16[128,256]{1,0:T(8,128)(2,1)S(1)} %bitcast.124), channel_id=1, replica_groups=mesh['parts'=2,'ctx'=8,'grp'=2] {'ctx'}, dimensions={0}, use_global_device_ids=true | all-gather | bytes 589824 | tf_op jit(solution)/shard_map/all_gather | solution.py:140
  61.4 27.0 %all-gather.1 = bf16[1,1024,256]{2,1,0:T(8,128)(2,1)S(1)} all-gather(bf16[1,128,256]{2,1,0:T(8,128)(2,1)} %param.19), channel_id=3, replica_groups=mesh['parts'=2,'ctx'=8,'grp'=2] {'ctx'}, dimensions={1}, use_global_device_ids=true | all-gather | bytes 589824 | tf_op jit(solution)/shard_map/all_gather | solution.py:141
  88.4 6.5 %conditional.1 = (f32[2,1024,128]{2,1,0:T(8,128)S(1)}, f32[2,1024]{1,0:T(2,128)S(1)}) conditional(s32[]{:T(128)} %bitcast.3, () %tuple.16, (s32[128]{0:T(128)S(1)}, s32[1024]{0:T(1024)S(1)}, s32[1,128]{1,0:T(1,128)S(1)}, bf16[2,8,128,128]{3,2,1,0:T(8,128)(2,1)S(1)}, bf16[1024,256]{1,0:T(8,128)(2,1)S(1)}, ...), branch_computations={%region_2.0_spmd, %region_3.5_spmd} | conditional | flops 1086715904 | bytes 24917008 | solution.py:149
  89.6 2.3 fusion
  92.0 2.8 fusion.2
  95.0 1.1 divide_convert_fusion
  96.1 2.0 copy.122
  98.1 4.5 %reduce-window.6 = s32[16,8,128]{2,1,0:T(8,128)S(1)} reduce-window(s32[16,8,128]{2,1,0:T(8,128)S(1)} %fusion.33, s32[]{:T(128)} %constant.54.clone.1), window={size=1x1x128 pad=0_0x0_0x127_0}, to_apply=%region_8.9 | reduce-window | flops 2080768 | bytes 131076 | tf_op jit(solution)/shard_map/reduce-window
  103.4 5.0 %fusion.27 = (f32[128]{0:T(128)S(1)}, bf16[128,2048]{1,0:T(8,128)(2,1)S(1)}) fusion(bf16[128,2048]{0,1:T(8,128)(2,1)} %bitcast.116, bf16[2048,2048]{1,0:T(8,128)(2,1)} %all-gather.4.cloned.1.call-done, bf16[1,128,2048]{2,1,0:T(8,128)(2,1)} %param.16), kind=kOutput, calls=%fused_computation.38 | convolution fusion | flops 1075314560 | bytes 9961984 | tf_op jit(solution)/shard_map/dot_general | solution.py:164
  110.1 9.8 %scatter_custom_fusion = bf16[1152,2048]{1,0:T(8,128)(2,1)} fusion(s32[1024]{0:T(1024)S(1)} %bitcast.131, bf16[]{:T(256)} %constant.52.clone.1, bf16[128,2048]{1,0:T(8,128)(2,1)} %fusion.28), kind=kCustom, calls=%fused_computation.23 | custom fusion | bytes 5242882 | tf_op jit(solution)/shard_map/scatter | solution.py:186
  119.8 128.3 %all_to_all.10 = bf16[16,72,2048]{2,1,0:T(8,128)(2,1)S(1)} all-to-all(bf16[16,72,2048]{2,1,0:T(8,128)(2,1)} %bitcast.109), channel_id=1, replica_groups=mesh['parts'=2,'ctx'=8,'grp'=2] {'ctx','grp'}, dimensions={0} | all-to-all | bytes 9437184 | tf_op jit(solution)/shard_map/all_to_all | solution.py:188
  248.1 3.9 fusion.22
  252.0 4.2 %fusion.19 = bf16[1152,768]{1,0:T(8,128)(2,1)S(1)} fusion(bf16[1152,2048]{1,0:T(8,128)(2,1)S(1)} %bitcast.113, f32[1152,768]{1,0:T(8,128)S(1)} %fusion.22, bf16[1,2048,768]{2,1,0:T(8,128)(2,1)S(1)} %copy-done.11), kind=kOutput, calls=%fused_computation.26 | convolution fusion | flops 3629187072 | bytes 13172736 | tf_op jit(solution)/shard_map/dot_general | solution.py:100
  256.2 5.5 %convolution_convert_fusion = bf16[1152,2048]{1,0:T(8,128)(2,1)} fusion(bf16[1152,768]{1,0:T(8,128)(2,1)S(1)} %fusion.19, bf16[1,768,2048]{2,1,0:T(8,128)(2,1)S(1)} %copy-done), kind=kOutput, calls=%fused_computation.20 | convolution fusion | flops 3626237952 | bytes 9633792 | tf_op jit(solution)/shard_map/dot_general | solution.py:102
  261.8 4.9 %all-to-all-start.1 = ((bf16[16,72,2048]{2,1,0:T(8,128)(2,1)}), bf16[16,72,2048]{2,1,0:T(8,128)(2,1)}, u32[]{:S(2)}, u32[]{:S(2)}) async-start(bf16[16,72,2048]{2,1,0:T(8,128)(2,1)} %bitcast.111), calls=%async_computation.1 | async-start | bytes 9437184 | tf_op jit(solution)/shard_map/all_to_all | solution.py:196
  266.7 1.3 fusion.34
  268.2 102.2 %all-to-all-done.1 = bf16[16,72,2048]{2,1,0:T(8,128)(2,1)} async-done(((bf16[16,72,2048]{2,1,0:T(8,128)(2,1)}), bf16[16,72,2048]{2,1,0:T(8,128)(2,1)}, u32[]{:S(2)}, u32[]{:S(2)}) %all-to-all-start.1) | async-done | bytes 4718624 | tf_op jit(solution)/shard_map/all_to_all | solution.py:196
  370.4 11.8 %gather_fusion.1 = bf16[1024,2048]{1,0:T(8,128)(2,1)} fusion(bf16[1152,2048]{1,0:T(8,128)(2,1)} %bitcast.28, s32[1024]{0:T(1024)S(1)} %broadcast_clamp_fusion), kind=kCustom, calls=%fused_computation.1 | custom fusion | bytes 8392704 | tf_op jit(solution)/shard_map/gather | solution.py:199
  382.2 3.5 fusion.15
  385.7 1.1 fusion.30
  (76 shorter events, 12.4 us)
Async XLA Ops:
  7.2 249.0 %copy-start = (bf16[1,768,2048]{2,1,0:T(8,128)(2,1)S(1)}, bf16[1,768,2048]{2,1,0:T(8,128)(2,1)}, u32[]{:S(2)}) copy-start(bf16[1,768,2048]{2,1,0:T(8,128)(2,1)} %param.27) | copy-start | bytes 9437188
  7.2 4.9 %copy-start.9 = (s32[64]{0:T(128)S(1)}, s32[64]{0:T(128)}, u32[]{:S(2)}) copy-start(s32[64]{0:T(128)} %constant.71) | copy-start | bytes 772
  7.2 4.8 %copy-start.8 = (s32[3,1,128]{2,1,0:T(1,128)S(1)}, s32[3,1,128]{2,1,0:T(1,128)}, u32[]{:S(2)}) copy-start(s32[3,1,128]{2,1,0:T(1,128)} %param.20) | copy-start | bytes 4612
  7.2 96.2 %all-gather.4.cloned.1.call-start = ((), (), s32[]{:S(2)}) async-start(), calls=%async_computation.2 | async-start | bytes 8912896 | tf_op jit(solution)/shard_map/all_gather | solution.py:166
  10.4 1.1 copy-start.1
  11.8 5.3 %copy-start.4 = (bf16[1,128,256]{2,1,0:T(8,128)(2,1)S(1)}, bf16[1,128,256]{2,1,0:T(8,128)(2,1)}, u32[]{:S(2)}) copy-start(bf16[1,128,256]{2,1,0:T(8,128)(2,1)} %param.18) | copy-start | bytes 196612
  13.1 6.2 %copy-start.7 = (s32[1,128]{1,0:T(1,128)S(1)}, s32[1,128]{1,0:T(1,128)}, u32[]{:S(2)}) copy-start(s32[1,128]{1,0:T(1,128)} %param.21) | copy-start | bytes 1540
  88.4 14.6 %copy-start.6 = (s32[1,128,8]{1,2,0:T(8,128)S(1)}, s32[1,128,8]{1,2,0:T(8,128)}, u32[]{:S(2)}) copy-start(s32[1,128,8]{1,2,0:T(8,128)} %param.22) | copy-start | bytes 12292
  108.3 0.8 copy-start.2
  119.8 128.3 %copy-start.10 = (bf16[1,2048,768]{2,1,0:T(8,128)(2,1)S(1)}, bf16[1,2048,768]{2,1,0:T(8,128)(2,1)}, u32[]{:S(2)}) copy-start(bf16[1,2048,768]{2,1,0:T(8,128)(2,1)} %param.25) | copy-start | bytes 9437188
  248.1 3.9 copy-start.11
  261.7 4.9 %copy-start.5 = (bf16[2048,16]{0,1:T(8,128)(2,1)S(1)}, bf16[2048,16]{0,1:T(8,128)(2,1)}, u32[]{:S(2)}) copy-start(bf16[2048,16]{0,1:T(8,128)(2,1)} %param.24) | copy-start | bytes 196612
  261.8 108.6 %all-to-all-start.1 = ((bf16[16,72,2048]{2,1,0:T(8,128)(2,1)}), bf16[16,72,2048]{2,1,0:T(8,128)(2,1)}, u32[]{:S(2)}, u32[]{:S(2)}) async-start(bf16[16,72,2048]{2,1,0:T(8,128)(2,1)} %bitcast.111), calls=%async_computation.1 | async-start | bytes 9437184 | tf_op jit(solution)/shard_map/all_to_all | solution.py:196
  382.2 3.5 copy-start.3
Sparse Core Ops, SparseCore 0:
  10.2 86.8 all-gather.3
where the time goes:
time: 394 us
  blocking collectives  196 us (50%)
  waiting for transfers between devices  103 us (26%)
  local copies, waits for them, and re-layouts  31.9 us (8%)
  matrix products  28.4 us (7%)
  between operations  15 us (4%)
  other arithmetic  14.4 us (4%)
  starting transfers between devices  4.96 us (1%)
    all_to_all x1, blocking collectives, on_device(): lax.all_to_all(send_rows.reshape(expert_count, capacity, D), ('ctx', 'grp...  128 us
    all_to_all x1, waiting for transfers between devices, on_device(): lax.all_to_all(produced.reshape(received.shape), ('ctx', 'grp'), split_ax...  102 us
    all_gather x1, blocking collectives, on_device(): lax.all_gather(key_rot, 'ctx', axis=0, tiled=True)  29.1 us
    all_gather x1, blocking collectives, on_device(): lax.all_gather(value_in[0], 'ctx', axis=0, tiled=True)  27 us
    gather x1, local copies, waits for them, and re-layouts, on_device(): answered.reshape(expert_count * capacity, D)[slot_place]  11.8 us
    all_gather x1, blocking collectives, on_device(): lax.all_gather(own_seg, 'ctx', axis=0, tiled=True)  11.6 us
    scatter x1, local copies, waits for them, and re-layouts, on_device(): send_rows = jnp.zeros((expert_count * capacity, D), jnp.bfloat16).at[slot...  9.76 us
  transfers between devices with their start and end apart: 2, of which 1 were waited for; matrix products, arithmetic and copies ran while one was open for 7% of the time, Pallas kernels for 0%

commit v1 on v0

--- a/solution.py
+++ b/solution.py
@@ -86,13 +86,6 @@
     )
     totals = jnp.sum(weights, axis=-1)
     return (weighted, totals)
-
-
-def route_gates(logits, flat_ids):
-    matches = flat_ids[:, :, None] == jnp.arange(logits.shape[1], dtype=jnp.int32)[None, None, :]
-    picked = jnp.sum(jnp.where(matches, logits[:, None, :], 0.0), axis=-1)
-    raised = jnp.exp(picked)
-    return raised / jnp.sum(raised, axis=-1, keepdims=True)
 
 
 def expert_mlp(rows_in, gate_mat, up_mat, down_mat):
@@ -168,36 +161,43 @@
     )
     residual = (hidden_in[0].astype(jnp.float32) + projected).astype(jnp.bfloat16)
     normed = row_norm(residual.astype(jnp.float32)).astype(jnp.bfloat16)
-    logits = jnp.dot(normed, w_router, preferred_element_type=jnp.float32)
     own_ids = expert_ids[0]
-    gates = route_gates(logits, own_ids)
     expert_count = w_router.shape[1]
     capacity = 9 * tokens * TOP // (8 * expert_count)
-    flat_ids = own_ids.reshape(-1)
-    matches = (flat_ids[:, None] == jnp.arange(expert_count, dtype=jnp.int32)[None, :]).astype(
-        jnp.int32
-    )
-    running_count = jnp.cumsum(matches, axis=0)
-    slot_rank = jnp.sum(matches * (running_count - 1), axis=1)
-    slot_place = flat_ids * capacity + slot_rank
-    send_rows = (
-        jnp.zeros((expert_count * capacity, D), jnp.bfloat16)
-        .at[slot_place]
-        .set(jnp.repeat(normed, TOP, axis=0))
-    )
-    received = lax.all_to_all(
-        send_rows.reshape(expert_count, capacity, D),
-        ("ctx", "grp"),
-        split_axis=0,
-        concat_axis=0,
-        tiled=True,
-    )
-    produced = expert_mlp(received.reshape(-1, D), w_gate[0], w_up[0], w_down[0])
-    answered = lax.all_to_all(
-        produced.reshape(received.shape), ("ctx", "grp"), split_axis=0, concat_axis=0, tiled=True
-    )
-    fetched = answered.reshape(expert_count * capacity, D)[slot_place].reshape(tokens, TOP, D)
-    mixture = jnp.einsum("tk,tkd->td", gates, fetched, preferred_element_type=jnp.float32)
+    places = ("ctx", "grp")
+    own_expert = lax.axis_index(places)
+    expert_range = jnp.arange(expert_count, dtype=jnp.int32)
+    chosen = jnp.any(own_ids[:, :, None] == expert_range[None, None, :], axis=1)
+    all_chosen = lax.all_gather(chosen.astype(jnp.bfloat16), places, axis=0, tiled=False)
+    all_rows = lax.all_gather(normed, places, axis=0, tiled=False)
+    blocks = all_rows.shape[0]
+    logits = jnp.einsum("btd,de->bte", all_rows, w_router, preferred_element_type=jnp.float32)
+    raised = jnp.where(all_chosen > 0, jnp.exp(logits), 0.0)
+    is_own = (expert_range == own_expert)[None, None, :]
+    own_gate = jnp.sum(jnp.where(is_own, raised, 0.0), axis=-1) / jnp.sum(raised, axis=-1)
+    routed = jnp.sum(jnp.where(is_own, all_chosen.astype(jnp.float32), 0.0), axis=-1)
+    earlier = jnp.tril(jnp.ones((tokens, tokens), jnp.float32), -1).astype(jnp.bfloat16)
+    rank = jnp.einsum(
+        "bt,st->bs", routed.astype(jnp.bfloat16), earlier, preferred_element_type=jnp.float32
+    )
+    slot = jnp.where(routed > 0, rank, -1.0).astype(jnp.int32)
+    slot_range = jnp.arange(capacity, dtype=jnp.int32)
+    picks = slot[:, None, :] == slot_range[None, :, None]
+    rows_in = jnp.einsum(
+        "bct,btd->bcd", picks.astype(jnp.bfloat16), all_rows, preferred_element_type=jnp.float32
+    ).astype(jnp.bfloat16)
+    row_gate = jnp.sum(jnp.where(picks, own_gate[:, None, :], 0.0), axis=-1)
+    produced = expert_mlp(rows_in.reshape(-1, D), w_gate[0], w_up[0], w_down[0])
+    scaled = (produced.astype(jnp.float32) * row_gate.reshape(-1, 1)).astype(jnp.bfloat16)
+    spread = jnp.einsum(
+        "bct,bcd->btd",
+        picks.astype(jnp.bfloat16),
+        scaled.reshape(blocks, capacity, D),
+        preferred_element_type=jnp.float32,
+    ).astype(jnp.bfloat16)
+    mixture = lax.psum_scatter(
+        spread.reshape(blocks * tokens, D), places, scatter_dimension=0, tiled=True
+    ).astype(jnp.float32)
     layer_out = (residual.astype(jnp.float32) + mixture).astype(jnp.bfloat16)
     return (residual[None], layer_out[None])
 

time: 394 us -> 339 us (0.86)
  blocking collectives: 196 us -> 104 us
  waiting for transfers between devices: 103 us -> 158 us
  local copies, waits for them, and re-layouts: 31.9 us -> 8.65 us
  matrix products: 28.4 us -> 40.3 us
  starting transfers between devices: 4.96 us -> 0.12 us
    all_to_all x1 -> x0, blocking collectives: 128 us -> none  [on_device(): lax.all_to_all(send_rows.reshape(expert_count, capacity, D), ('ctx', 'grp...]
    reduce_scatter x0 -> x1, waiting for transfers between devices: none -> 103 us  [on_device(): lax.psum_scatter(spread.reshape(blocks * tokens, D), places, scatter_dime...]
    all_to_all x1 -> x0, waiting for transfers between devices: 102 us -> none  [on_device(): lax.all_to_all(produced.reshape(received.shape), ('ctx', 'grp'), split_ax...]
    all_gather x0 -> x1, waiting for transfers between devices: none -> 54.7 us  [on_device(): all_rows = lax.all_gather(normed, places, axis=0, tiled=False)]
    all_gather x0 -> x1, blocking collectives: none -> 36.2 us  [on_device(): lax.all_gather(chosen.astype(jnp.bfloat16), places, axis=0, tiled=False)]
    gather x1 -> x0, local copies, waits for them, and re-layouts: 11.8 us -> none  [on_device(): answered.reshape(expert_count * capacity, D)[slot_place]]
    dot_general x2 -> x4, matrix products: 4.75 us -> 15.2 us  [the longest x1 5.83 us: on_device(): jnp.einsum('btd,de->bte', all_rows, w_router, preferred_element_type=jnp....]
    scatter x1 -> x0, local copies, waits for them, and re-layouts: 9.76 us -> none  [on_device(): send_rows = jnp.zeros((expert_count * capacity, D), jnp.bfloat16).at[slot...]
  transfers between devices with their start and end apart: 2 -> 3, of which waited for: 1 -> 3; matrix products, arithmetic and copies ran while one was open for 7% -> 6% of each run, Pallas kernels for 0% -> 0%
where the time goes in v1:
time: 339 us; the launch traced here: 337 us
  waiting for transfers between devices  158 us (47%)
  blocking collectives  104 us (31%)
  matrix products  40.3 us (12%)
  between operations  14.7 us (4%)
  other arithmetic  11.2 us (3%)
  local copies, waits for them, and re-layouts  8.65 us (3%)
    reduce_scatter x1, waiting for transfers between devices, on_device(): lax.psum_scatter(spread.reshape(blocks * tokens, D), places, scatter_dime...  103 us
    all_gather x1, waiting for transfers between devices, on_device(): all_rows = lax.all_gather(normed, places, axis=0, tiled=False)  54.7 us
    all_gather x1, blocking collectives, on_device(): lax.all_gather(chosen.astype(jnp.bfloat16), places, axis=0, tiled=False)  36.2 us
    all_gather x1, blocking collectives, on_device(): lax.all_gather(key_rot, 'ctx', axis=0, tiled=True)  29 us
    all_gather x1, blocking collectives, on_device(): lax.all_gather(value_in[0], 'ctx', axis=0, tiled=True)  26.3 us
    all_gather x1, blocking collectives, on_device(): lax.all_gather(own_seg, 'ctx', axis=0, tiled=True)  12 us
  transfers between devices with their start and end apart: 3, of which 3 were waited for; matrix products, arithmetic and copies ran while one was open for 6% of the time, Pallas kernels for 0%

profile of v1, /device:TPU:15, one launch (start us, length us, event | category | flops | bytes accessed | tf_op | source)
XLA Modules:
  0.0 336.8 jit_solution(17662359205430079255)
XLA Ops:
  8.0 1.3 convert_bitcast_fusion
  9.5 1.0 copy-done.3
  12.2 1.6 broadcast_multiply_fusion
  18.3 12.0 %all-gather = s32[1,1024]{1,0:T(1,128)S(1)} all-gather(s32[1,128]{1,0:T(1,128)S(1)} %copy-done.8), channel_id=2, replica_groups=mesh['parts'=2,'ctx'=8,'grp'=2] {'ctx'}, dimensions={1}, use_global_device_ids=true | all-gather | bytes 4608 | tf_op jit(solution)/shard_map/all_gather | solution.py:135
  30.3 1.5 maximum_bitcast_fusion
  31.8 29.0 %all_gather.23 = bf16[1024,256]{1,0:T(8,128)(2,1)S(1)} all-gather(bf16[128,256]{1,0:T(8,128)(2,1)S(1)} %bitcast.115), channel_id=1, replica_groups=mesh['parts'=2,'ctx'=8,'grp'=2] {'ctx'}, dimensions={0}, use_global_device_ids=true | all-gather | bytes 589824 | tf_op jit(solution)/shard_map/all_gather | solution.py:133
  60.8 26.3 %all-gather.1 = bf16[1,1024,256]{2,1,0:T(8,128)(2,1)S(1)} all-gather(bf16[1,128,256]{2,1,0:T(8,128)(2,1)} %param.19), channel_id=3, replica_groups=mesh['parts'=2,'ctx'=8,'grp'=2] {'ctx'}, dimensions={1}, use_global_device_ids=true | all-gather | bytes 589824 | tf_op jit(solution)/shard_map/all_gather | solution.py:134
  87.2 6.4 %conditional.1 = (f32[2,1024,128]{2,1,0:T(8,128)S(1)}, f32[2,1024]{1,0:T(2,128)S(1)}) conditional(s32[]{:T(128)} %bitcast.3, () %tuple.16, (s32[128]{0:T(128)S(1)}, s32[1024]{0:T(1024)S(1)}, s32[1,128]{1,0:T(1,128)S(1)}, bf16[2,8,128,128]{3,2,1,0:T(8,128)(2,1)S(1)}, bf16[1024,256]{1,0:T(8,128)(2,1)S(1)}, ...), branch_computations={%region_2.0_spmd, %region_3.5_spmd} | conditional | flops 1086715904 | bytes 24917008 | solution.py:142
  88.4 2.3 fusion
  90.7 2.8 fusion.2
  93.5 1.1 divide_convert_fusion
  94.7 2.0 copy.101
  96.9 5.0 %fusion.23 = (f32[128]{0:T(128)S(1)}, bf16[128,2048]{1,0:T(8,128)(2,1)S(1)}) fusion(bf16[128,2048]{0,1:T(8,128)(2,1)} %bitcast.107, bf16[2048,2048]{1,0:T(8,128)(2,1)} %all-gather.7.cloned.1.call-done, bf16[1,128,2048]{2,1,0:T(8,128)(2,1)} %param.16), kind=kOutput, calls=%fused_computation.37 | convolution fusion | flops 1075314560 | bytes 9961984 | tf_op jit(solution)/shard_map/dot_general | solution.py:157
  102.7 0.9 fusion.24
  103.8 36.2 %all-gather.2 = bf16[2048,16]{0,1:T(8,128)(2,1)S(1)} all-gather(bf16[128,16]{0,1:T(8,128)(2,1)S(1)} %convert_element_type.164), channel_id=4, replica_groups=mesh['parts'=2,'ctx'=8,'grp'=2] {'ctx','grp'}, dimensions={0}, use_global_device_ids=true | all-gather | bytes 69632 | tf_op jit(solution)/shard_map/all_gather | solution.py:171
  140.0 54.7 %all-gather.9.cloned.1.call-done = bf16[2048,2048]{1,0:T(8,128)(2,1)} async-done(((bf16[128,2048]{1,0:T(8,128)(2,1)}), bf16[2048,2048]{1,0:T(8,128)(2,1)}) %all-gather.9.cloned.1.call-update) | async-done | bytes 8388624 | tf_op jit(solution)/shard_map/all_gather | solution.py:172
  194.7 5.8 %fusion.38 = (f32[16,128]{1,0:T(8,128)S(1)}, f32[16,128]{1,0:T(8,128)S(1)}, f32[16,128]{1,0:T(8,128)S(1)}) fusion(pred[16]{0:T(512)(128)(4,1)S(1)} %iota_compare_fusion.6, bf16[16,128,2048]{2,1,0:T(8,128)(2,1)} %bitcast.97, bf16[2048,16]{0,1:T(8,128)(2,1)S(1)} %copy-done.5, bf16[2048,16]{0,1:T(8,128)(2,1)S(1)} %all-gather.2), kind=kOutput, calls=%fused_computation.86 | convolution fusion | flops 134473728 | bytes 8544272 | tf_op jit(solution)/shard_map/btd,de->bte/dot_general | solution.py:174
  200.7 3.5 %convolution_convert_fusion.2 = bf16[16,72,2048]{2,1,0:T(8,128)(2,1)} fusion(bf16[16,128,2048]{2,1,0:T(8,128)(2,1)S(1)} %bitcast.98, s32[16,128]{1,0:T(8,128)S(1)} %fusion.22), kind=kOutput, calls=%fused_computation.22 | convolution fusion | flops 606486528 | bytes 13115392 | tf_op jit(solution)/shard_map/bct,btd->bcd/dot_general | solution.py:186
  204.8 6.8 %fusion.18 = f32[1152,768]{1,0:T(8,128)S(1)} fusion(bf16[1152,2048]{1,0:T(8,128)(2,1)} %bitcast.101, bf16[1,2048,768]{2,1,0:T(8,128)(2,1)} %param.25), kind=kOutput, calls=%fused_computation.26 | convolution fusion | flops 3623878656 | bytes 11403264 | tf_op jit(solution)/shard_map/dot_general | solution.py:92
  211.5 4.2 %fusion.15 = bf16[1152,768]{1,0:T(8,128)(2,1)S(1)} fusion(bf16[1152,2048]{1,0:T(8,128)(2,1)S(1)} %bitcast.102, f32[1152,768]{1,0:T(8,128)S(1)} %fusion.18, bf16[1,2048,768]{2,1,0:T(8,128)(2,1)S(1)} %copy-done.11), kind=kOutput, calls=%fused_computation.23 | convolution fusion | flops 3629187072 | bytes 13172736 | tf_op jit(solution)/shard_map/dot_general | solution.py:93
  215.7 4.1 %multiply_convert_fusion = bf16[1152,2048]{1,0:T(8,128)(2,1)S(1)} fusion(bf16[1152,768]{1,0:T(8,128)(2,1)S(1)} %fusion.15, f32[1152]{0:T(1024)S(1)} %mul.171, bf16[1,768,2048]{2,1,0:T(8,128)(2,1)S(1)} %copy-done), kind=kOutput, calls=%fused_computation.18 | convolution fusion | flops 3633315840 | bytes 9638400 | tf_op jit(solution)/shard_map/dot_general | solution.py:95
  219.8 5.6 %convolution_convert_fusion.1 = bf16[16,128,2048]{2,1,0:T(8,128)(2,1)} fusion(bf16[16,72,2048]{2,1,0:T(8,128)(2,1)S(1)} %bitcast.105, s32[16,128]{1,0:T(8,128)S(1)} %fusion.22), kind=kOutput, calls=%fused_computation.20 | convolution fusion | flops 608321536 | bytes 13115392 | tf_op jit(solution)/shard_map/bct,bcd->btd/dot_general | solution.py:192
  225.5 102.7 %reduce-scatter.2.cloned.1.call-done = bf16[128,2048]{1,0:T(8,128)(2,1)} async-done(((bf16[2048,2048]{1,0:T(8,128)(2,1)}), bf16[128,2048]{1,0:T(8,128)(2,1)}) %reduce-scatter.2.cloned.1.call-update) | async-done | bytes 524304 | tf_op jit(solution)/shard_map/reduce_scatter | solution.py:198
  328.2 2.1 fusion.26
  (66 shorter events, 9.4 us)
Async XLA Ops:
  7.2 208.6 %copy-start = (bf16[1,768,2048]{2,1,0:T(8,128)(2,1)S(1)}, bf16[1,768,2048]{2,1,0:T(8,128)(2,1)}, u32[]{:S(2)}) copy-start(bf16[1,768,2048]{2,1,0:T(8,128)(2,1)} %param.27) | copy-start | bytes 9437188
  7.2 3.9 %copy-start.10 = (s32[64]{0:T(128)S(1)}, s32[64]{0:T(128)}, u32[]{:S(2)}) copy-start(s32[64]{0:T(128)} %constant.73) | copy-start | bytes 772
  7.2 3.9 %copy-start.9 = (s32[3,1,128]{2,1,0:T(1,128)S(1)}, s32[3,1,128]{2,1,0:T(1,128)}, u32[]{:S(2)}) copy-start(s32[3,1,128]{2,1,0:T(1,128)} %param.20) | copy-start | bytes 4612
  7.2 89.7 %all-gather.7.cloned.1.call-start = ((), (), s32[]{:S(2)}) async-start(), calls=%async_computation.1 | async-start | bytes 8912896 | tf_op jit(solution)/shard_map/all_gather | solution.py:159
  7.9 186.8 %all-gather.9.cloned.1.call-start = ((), (), s32[]{:S(2)}) async-start(), calls=%async_computation.3 | async-start | bytes 8912896 | tf_op jit(solution)/shard_map/all_gather | solution.py:172
  9.5 1.1 copy-start.3
  9.5 6.7 %copy-start.6 = (bf16[1,128,256]{2,1,0:T(8,128)(2,1)S(1)}, bf16[1,128,256]{2,1,0:T(8,128)(2,1)}, u32[]{:S(2)}) copy-start(bf16[1,128,256]{2,1,0:T(8,128)(2,1)} %param.18) | copy-start | bytes 196612
  11.9 6.4 %copy-start.8 = (s32[1,128]{1,0:T(1,128)S(1)}, s32[1,128]{1,0:T(1,128)}, u32[]{:S(2)}) copy-start(s32[1,128]{1,0:T(1,128)} %param.21) | copy-start | bytes 1540
  96.9 6.8 %copy-start.7 = (s32[1,128,8]{1,2,0:T(8,128)S(1)}, s32[1,128,8]{1,2,0:T(8,128)}, u32[]{:S(2)}) copy-start(s32[1,128,8]{1,2,0:T(8,128)} %param.22) | copy-start | bytes 12292
  96.9 97.8 %copy-start.5 = (bf16[2048,16]{0,1:T(8,128)(2,1)S(1)}, bf16[2048,16]{0,1:T(8,128)(2,1)}, u32[]{:S(2)}) copy-start(bf16[2048,16]{0,1:T(8,128)(2,1)} %param.24) | copy-start | bytes 196612
  101.9 0.8 copy-start.4
  103.7 224.5 %reduce-scatter.2.cloned.1.call-start = ((), (), s32[]{:S(2)}) async-start(), calls=%async_computation.2 | async-start | bytes 8912896 | tf_op jit(solution)/shard_map/reduce_scatter | solution.py:198
  194.7 6.0 %copy-start.1 = (bf16[2048,2048]{1,0:T(8,128)(2,1)S(1)}, bf16[2048,2048]{1,0:T(8,128)(2,1)}, u32[]{:S(2)}) copy-start(bf16[2048,2048]{1,0:T(8,128)(2,1)} %all-gather.9.cloned.1.call-done) | copy-start | bytes 25165828
  204.7 6.8 %copy-start.2 = (bf16[16,72,2048]{2,1,0:T(8,128)(2,1)S(1)}, bf16[16,72,2048]{2,1,0:T(8,128)(2,1)}, u32[]{:S(2)}) copy-start(bf16[16,72,2048]{2,1,0:T(8,128)(2,1)} %convolution_convert_fusion.2) | copy-start | bytes 14155780
  204.7 6.8 %copy-start.11 = (bf16[1,2048,768]{2,1,0:T(8,128)(2,1)S(1)}, bf16[1,2048,768]{2,1,0:T(8,128)(2,1)}, u32[]{:S(2)}) copy-start(bf16[1,2048,768]{2,1,0:T(8,128)(2,1)} %param.26) | copy-start | bytes 9437188
Sparse Core Ops, SparseCore 0:
  10.2 86.6 all-gather.6
  103.8 90.8 all-gather.8
  225.6 102.5 reduce-scatter.1

commit v2 on v1

--- a/solution.py
+++ b/solution.py
@@ -1,9 +1,12 @@
+import functools
 import math
 
 import jax
 import jax.numpy as jnp
 import numpy as np
 from jax import lax
+from jax.experimental import pallas as pl
+from jax.experimental.pallas import tpu as pltpu
 from jax.sharding import PartitionSpec as P
 
 D = 2048
@@ -93,6 +96,500 @@
     up_part = jnp.dot(rows_in, up_mat, preferred_element_type=jnp.float32)
     acts = (jax.nn.silu(gate_part) * up_part).astype(jnp.bfloat16)
     return jnp.dot(acts, down_mat, preferred_element_type=jnp.float32).astype(jnp.bfloat16)
+
+
+META = 128
+MESH = pl.DeviceIdType.MESH
+VMEM_MOST = 64 * 1000 * 1024
+NT = (((1,), (1,)), ((), ()))
+TN = (((0,), (0,)), ((), ()))
+
+
+def ring_place(index, n):
+    odd = index % 2
+    return (1 - odd) * (index // 2) + odd * (n - 1 - index // 2)
+
+
+def ring_index(place, n):
+    place = (place + 2 * n) % n
+    back = place // (n // 2)
+    return (1 - back) * (2 * place) + back * (2 * (n - 1 - place) + 1)
+
+
+def remote(src, dst, sems, slot, where):
+    return pltpu.make_async_remote_copy(
+        src_ref=src,
+        dst_ref=dst,
+        send_sem=sems.at[0, slot],
+        recv_sem=sems.at[1, slot],
+        device_id=where,
+        device_id_type=MESH,
+    )
+
+
+def greet(wheres):
+    barrier = pltpu.get_barrier_semaphore()
+    for where in wheres:
+        pl.semaphore_signal(barrier, inc=1, device_id=where, device_id_type=MESH)
+    pl.semaphore_wait(barrier, len(wheres))
+
+
+def attend_kernel(n, q_ref, kv_ref, w_ref, hid_ref, res_ref, kv_all, w_all, att, kv_sem, w_sem, p_sem, own_sem):
+    ctx = lax.axis_index("ctx")
+    grp = lax.axis_index("grp")
+    place = ring_place(ctx, n)
+    far = n // 2
+    tokens = q_ref.shape[0]
+    rows = w_ref.shape[0]
+    toward = [{"ctx": ring_index(place + 1, n)}, {"ctx": ring_index(place - 1, n)}]
+    partner = {"grp": 1 - grp}
+    greet(toward + [partner])
+
+    def source(side, hop):
+        return ring_index(place - hop if side == 0 else place + hop, n)
+
+    def half(ref, part):
+        size = ref.shape[0] // 2
+        return ref.at[pl.ds(part * size, size)]
+
+    def kv_copy(side, part, hop):
+        owner = source(side, hop)
+        block = half(kv_all.at[pl.ds(pl.multiple_of(owner * tokens, tokens), tokens)], part)
+        src = half(kv_ref, part) if isinstance(hop, int) and hop == 0 else block
+        return remote(src, block, kv_sem, (side * 2 + part) * far + hop, toward[side])
+
+    def w_block(owner, which, part):
+        start = pl.multiple_of((owner * 2 + which) * rows, rows)
+        return half(w_all.at[pl.ds(start, rows)], part)
+
+    def w_copy(side, part, hop):
+        block = w_block(source(side, hop), grp, part)
+        src = half(w_ref, part) if isinstance(hop, int) and hop == 0 else block
+        return remote(src, block, w_sem, (side * 2 + part) * far + hop, toward[side])
+
+    def p_copy(side, part, hop):
+        block = w_block(source(side, hop), grp, part)
+        src = half(w_ref, part) if isinstance(hop, int) and hop == 0 else block
+        return remote(src, block, p_sem, (side * 2 + part) * (far + 1) + hop, partner)
+
+    def hops(side, part):
+        return far if part == side else far - 1
+
+    started, passed = [], []
+
+    def launch(make, side, part, hop):
+        if hop < hops(side, part):
+            copy = make(side, part, hop)
+            copy.start()
+            started.append(copy)
+
+    def pass_on(side, part, hop):
+        copy = p_copy(side, part, hop)
+        copy.start()
+        passed.append(copy)
+
+    def kv_step(hop):
+        for side in range(2):
+            for part in (side, 1 - side):
+                if hop <= hops(side, part):
+                    kv_copy(side, part, hop - 1).wait_recv()
+                    launch(kv_copy, side, part, hop)
+
+    def w_step(hop, lead):
+        for side in range(2):
+            part = side if lead else 1 - side
+            if hop <= hops(side, part):
+                w_copy(side, part, hop - 1).wait_recv()
+                launch(w_copy, side, part, hop)
+                pass_on(side, part, hop)
+
+    own_kv = pltpu.make_async_copy(
+        kv_ref, kv_all.at[pl.ds(pl.multiple_of(ctx * tokens, tokens), tokens)], own_sem.at[0]
+    )
+    own_w = pltpu.make_async_copy(
+        w_ref, w_all.at[pl.ds(pl.multiple_of((ctx * 2 + grp) * rows, rows), rows)], own_sem.at[1]
+    )
+    own_kv.start()
+    own_w.start()
+    for side in range(2):
+        for part in range(2):
+            launch(kv_copy, side, part, 0)
+    events = [(hop, lead) for hop in range(far + 1) for lead in (True, False)]
+    for side in range(2):
+        launch(w_copy, side, side, 0)
+    for part in range(2):
+        pass_on(0, part, 0)
+    done = 1
+    for hop in range(1, far + 1):
+        kv_step(hop)
+        hop_w, lead = events[done]
+        if hop_w == 0:
+            for side in range(2):
+                launch(w_copy, side, 1 - side, 0)
+        else:
+            w_step(hop_w, lead)
+        done += 1
+    own_kv.wait()
+    group = HEADS // KV_HEADS
+    width = KV_HEADS * HD
+    keys = kv_all.shape[0]
+    pick_one = (lax.broadcasted_iota(jnp.int32, (8, META), 1) == 0).astype(jnp.bfloat16)
+    seg_of_key = lax.dot_general(
+        pick_one, kv_all[:, 2 * width :], NT, preferred_element_type=jnp.float32
+    )[0:1]
+    seg_of_query = kv_ref[:, 2 * width : 2 * width + 1].astype(jnp.float32)
+    key_pos = lax.broadcasted_iota(jnp.int32, (tokens, keys), 1)
+    query_pos = lax.broadcasted_iota(jnp.int32, (tokens, keys), 0) + ctx * tokens
+    allowed = (key_pos <= query_pos) & (seg_of_key == seg_of_query)
+
+    def attend_heads(first, last):
+        @pl.loop(first, last)
+        def _(head):
+            at = pl.ds(pl.multiple_of(head * HD, HD), HD)
+            k_at = pl.ds(pl.multiple_of((head // group) * HD, HD), HD)
+            v_at = pl.ds(pl.multiple_of(width + (head // group) * HD, HD), HD)
+            scores = lax.dot_general(
+                q_ref[:, at], kv_all[:, k_at], NT, preferred_element_type=jnp.float32
+            ) * (1.0 / math.sqrt(HD))
+            weights = jnp.where(allowed, jnp.exp(scores), 0.0)
+            total = jnp.sum(weights, axis=-1, keepdims=True)
+            weighted = jnp.dot(
+                weights.astype(jnp.bfloat16), kv_all[:, v_at], preferred_element_type=jnp.float32
+            )
+            att[:, at] = (weighted / total).astype(jnp.bfloat16)
+
+    rest = events[done:]
+    pieces = 4
+    for piece in range(pieces):
+        attend_heads(piece * HEADS // pieces, (piece + 1) * HEADS // pieces)
+        if rest:
+            w_step(*rest.pop(0))
+    for event in rest:
+        w_step(*event)
+    own_w.wait()
+    for copy in passed:
+        copy.wait_recv()
+    tile = 512
+
+    @pl.loop(0, res_ref.shape[1] // tile)
+    def _(index):
+        at = pl.ds(pl.multiple_of(index * tile, tile), tile)
+        projected = jnp.dot(att[...], w_all[:, at], preferred_element_type=jnp.float32)
+        res_ref[:, at] = (hid_ref[:, at].astype(jnp.float32) + projected).astype(jnp.bfloat16)
+
+    for copy in started + passed:
+        copy.wait_send()
+
+
+def attend_project(n, query_rot, kv_rows, w_out, hidden):
+    tokens, keys, far = query_rot.shape[0], n * query_rot.shape[0], n // 2
+    vmem = pl.BlockSpec(memory_space=pltpu.VMEM)
+    return pl.pallas_call(
+        functools.partial(attend_kernel, n),
+        out_shape=jax.ShapeDtypeStruct(hidden.shape, jnp.bfloat16),
+        in_specs=[vmem] * 4,
+        out_specs=vmem,
+        scratch_shapes=[
+            pltpu.VMEM((keys, kv_rows.shape[1]), jnp.bfloat16),
+            pltpu.VMEM((2 * n * w_out.shape[0], w_out.shape[1]), jnp.bfloat16),
+            pltpu.VMEM(query_rot.shape, jnp.bfloat16),
+            pltpu.SemaphoreType.DMA((2, 4 * far)),
+            pltpu.SemaphoreType.DMA((2, 4 * far)),
+            pltpu.SemaphoreType.DMA((2, 4 * (far + 1))),
+            pltpu.SemaphoreType.DMA((2,)),
+        ],
+        compiler_params=pltpu.CompilerParams(
+            collective_id=0, has_side_effects=True, vmem_limit_bytes=40 * 1024 * 1024
+        ),
+    )(query_rot, kv_rows, w_out, hidden)
+
+
+def expert_kernel(
+    n, cap, x_ref, wg_hbm, wu_hbm, wd_hbm, out_ref,
+    x_all, wg, wu, wd, picks, rows_in, acts, scaled, gate_of, mine, other, theirs,
+    r_out, r_in, a_sem, p_sem, s_sem, r_sem, l_sem,
+):
+    ctx = lax.axis_index("ctx")
+    grp = lax.axis_index("grp")
+    place = ring_place(ctx, n)
+    far = n // 2
+    tokens = x_ref.shape[0]
+    size = tokens // 2
+    width = out_ref.shape[1]
+    experts = 2 * n
+    toward = [{"ctx": ring_index(place + 1, n)}, {"ctx": ring_index(place - 1, n)}]
+    partner = {"grp": 1 - grp}
+    greet(toward + [partner])
+
+    def source(side, hop):
+        return ring_index(place - hop if side == 0 else place + hop, n)
+
+    def part_of(ref, part):
+        return ref.at[pl.ds(part * size, size)]
+
+    def hops(side, part):
+        return far if part == side else far - 1
+
+    def a_copy(side, part, hop):
+        block = part_of(x_all.at[source(side, hop) * 2 + grp], part)
+        src = part_of(x_ref, part) if isinstance(hop, int) and hop == 0 else block
+        return remote(src, block, a_sem, (side * 2 + part) * far + hop, toward[side])
+
+    def p_copy(side, part, hop):
+        block = part_of(x_all.at[source(side, hop) * 2 + grp], part)
+        src = part_of(x_ref, part) if isinstance(hop, int) and hop == 0 else block
+        return remote(src, block, p_sem, (side * 2 + part) * (far + 1) + hop, partner)
+
+    def s_copy(chip, slot):
+        return remote(other.at[chip], theirs.at[chip], s_sem, slot, partner)
+
+    for side in range(2):
+        a_copy(side, side, 0).start()
+    for side in range(2):
+        a_copy(side, 1 - side, 0).start()
+    for part in range(2):
+        p_copy(0, part, 0).start()
+    own_x = pltpu.make_async_copy(x_ref, x_all.at[ctx * 2 + grp], l_sem.at[0])
+    loads = [own_x] + [
+        pltpu.make_async_copy(src.at[0], dst, l_sem.at[1 + at])
+        for at, (src, dst) in enumerate(((wg_hbm, wg), (wu_hbm, wu), (wd_hbm, wd)))
+    ]
+    for load in loads:
+        load.start()
+    for load in loads:
+        load.wait()
+
+    lane = lax.broadcasted_iota(jnp.int32, (8, META), 1)
+    line = lax.broadcasted_iota(jnp.int32, (8, META), 0)
+    select = (lane == line * experts + ctx * 2 + grp).astype(jnp.bfloat16)
+    earlier = (
+        lax.broadcasted_iota(jnp.int32, (tokens, tokens), 0)
+        < lax.broadcasted_iota(jnp.int32, (tokens, tokens), 1)
+    ).astype(jnp.bfloat16)
+    slot_at = lax.broadcasted_iota(jnp.int32, (cap, tokens), 0)
+    tile = 256
+
+    @pl.loop(0, far)
+    def _(step):
+        hop = step + 1
+        for lead in (True, False):
+            for side in range(2):
+                part = side if lead else 1 - side
+
+                def take(side=side, part=part, lead=lead):
+                    a_copy(side, part, hop - 1).wait_recv()
+                    p_copy(side, part, hop).start()
+
+                    @pl.when(hop < hops(side, part))
+                    def _():
+                        a_copy(side, part, hop).start()
+
+                if lead:
+                    take()
+                else:
+                    pl.when(hop < far)(take)
+        p_copy(0, 0, hop).wait_recv()
+
+        @pl.when(hop < far)
+        def _():
+            p_copy(0, 1, hop).wait_recv()
+
+        @pl.when(hop == far)
+        def _():
+            p_copy(1, 1, far).wait_recv()
+
+        @pl.when(step == 0)
+        def _():
+            p_copy(0, 0, 0).wait_recv()
+            p_copy(0, 1, 0).wait_recv()
+
+        @pl.when(step > 0)
+        def _():
+            p_copy(1, 0, step).wait_recv()
+            p_copy(1, 1, step).wait_recv()
+
+        chips = [source(0, hop), source(1, step)]
+        for at in range(4):
+            block = chips[at // 2] * 2 + at % 2
+            span = pl.ds(at * cap, cap)
+            meta = x_all[block, :, width:]
+            lines = lax.dot_general(select, meta, NT, preferred_element_type=jnp.float32)
+            gate_row = lines[0:1] + lines[1:2]
+            chosen = lines > 0.0
+            rank = jnp.dot(
+                chosen.astype(jnp.float32).astype(jnp.bfloat16),
+                earlier,
+                preferred_element_type=jnp.float32,
+            )
+            slot = jnp.where(chosen, rank, -1.0).astype(jnp.int32)[0:1]
+            here = slot_at == slot
+            picks[span] = here.astype(jnp.float32).astype(jnp.bfloat16)
+            gate_of[span] = jnp.sum(jnp.where(here, gate_row, 0.0), axis=-1, keepdims=True)
+
+            @pl.loop(0, width // 512)
+            def _(index):
+                cols = pl.ds(pl.multiple_of(index * 512, 512), 512)
+                rows_in[span, cols] = jnp.dot(
+                    picks[span], x_all[block, :, cols], preferred_element_type=jnp.float32
+                ).astype(jnp.bfloat16)
+
+        @pl.loop(0, wg.shape[1] // tile)
+        def _(index):
+            cols = pl.ds(pl.multiple_of(index * tile, tile), tile)
+            gate_part = jnp.dot(rows_in[...], wg[:, cols], preferred_element_type=jnp.float32)
+            up_part = jnp.dot(rows_in[...], wu[:, cols], preferred_element_type=jnp.float32)
+            silu = gate_part / (1.0 + jnp.exp(-gate_part))
+            acts[:, cols] = (silu * up_part).astype(jnp.bfloat16)
+
+        @pl.loop(0, width // tile)
+        def _(index):
+            cols = pl.ds(pl.multiple_of(index * tile, tile), tile)
+            produced = jnp.dot(acts[...], wd[:, cols], preferred_element_type=jnp.float32)
+            weighted = (produced * gate_of[...]).astype(jnp.bfloat16)
+            for at in range(4):
+                spread = lax.dot_general(
+                    picks[at * cap : (at + 1) * cap],
+                    weighted[at * cap : (at + 1) * cap],
+                    TN,
+                    preferred_element_type=jnp.float32,
+                ).astype(jnp.bfloat16)
+                scaled[at, :, cols] = spread
+
+        for at in range(2):
+            mine[chips[at]] = scaled[at * 2 + grp]
+            other[chips[at]] = scaled[at * 2 + 1 - grp]
+        for at in range(2):
+            s_copy(chips[at], at * far + step).start()
+
+    def taken(slot_side, step):
+        chip = source(0, step + 1) if slot_side == 0 else source(1, step)
+        s_copy(chip, slot_side * far + step).wait_recv()
+
+    def ready(place_off):
+        hop = place_off % n
+        if hop < far:
+            taken(1, hop)
+        else:
+            taken(0, n - hop - 1)
+
+    def pair_sum(place_off, part):
+        chip = ring_index(place + place_off, n)
+        span = pl.ds(part * size, size)
+        return mine[chip, span, :].astype(jnp.float32) + theirs[chip, span, :].astype(jnp.float32)
+
+    def r_copy(side, part, hop):
+        slot = (side * 2 + part) * far + hop
+        return remote(r_out.at[slot], r_in.at[slot], r_sem, slot, toward[side])
+
+    seen = set()
+
+    def sum_of(place_off, part):
+        if place_off % n not in seen:
+            seen.add(place_off % n)
+            ready(place_off)
+        return pair_sum(place_off, part)
+
+    for hop in range(far):
+        for lead in (True, False):
+            for side in range(2):
+                part = side if lead else 1 - side
+                total = hops(side, part)
+                if hop < total:
+                    away = total - hop
+                    value = sum_of(away if side == 0 else -away, part)
+                    slot = (side * 2 + part) * far + hop
+                    if hop > 0:
+                        r_copy(side, part, hop - 1).wait_recv()
+                        value = value + r_in[slot - 1].astype(jnp.float32)
+                    r_out[slot] = value.astype(jnp.bfloat16)
+                    r_copy(side, part, hop).start()
+    for part in range(2):
+        value = sum_of(0, part)
+        for side in range(2):
+            last = hops(side, part) - 1
+            r_copy(side, part, last).wait_recv()
+            value = value + r_in[(side * 2 + part) * far + last].astype(jnp.float32)
+        out_ref[part * size : (part + 1) * size, :] = value
+    for side in range(2):
+        for part in range(2):
+            for hop in range(hops(side, part)):
+                a_copy(side, part, hop).wait_send()
+                r_copy(side, part, hop).wait_send()
+            for hop in range(1, hops(side, part) + 1):
+                p_copy(side, part, hop).wait_send()
+    for part in range(2):
+        p_copy(0, part, 0).wait_send()
+    for step in range(far):
+        s_copy(source(0, step + 1), step).wait_send()
+        s_copy(source(1, step), far + step).wait_send()
+
+
+def expert_layer(n, cap, packed, w_gate, w_up, w_down):
+    tokens, far = packed.shape[0], n // 2
+    ff = w_gate.shape[2]
+    vmem = pl.BlockSpec(memory_space=pltpu.VMEM)
+    hbm = pl.BlockSpec(memory_space=pl.ANY)
+    bf = jnp.bfloat16
+    size = tokens // 2
+    return pl.pallas_call(
+        functools.partial(expert_kernel, n, cap),
+        out_shape=jax.ShapeDtypeStruct((tokens, D), jnp.float32),
+        in_specs=[vmem, hbm, hbm, hbm],
+        out_specs=vmem,
+        scratch_shapes=[
+            pltpu.VMEM((2 * n, tokens, packed.shape[1]), bf),
+            pltpu.VMEM((D, ff), bf),
+            pltpu.VMEM((D, ff), bf),
+            pltpu.VMEM((ff, D), bf),
+            pltpu.VMEM((4 * cap, tokens), bf),
+            pltpu.VMEM((4 * cap, D), bf),
+            pltpu.VMEM((4 * cap, ff), bf),
+            pltpu.VMEM((4, tokens, D), bf),
+            pltpu.VMEM((4 * cap, 1), jnp.float32),
+            pltpu.VMEM((n, tokens, D), bf),
+            pltpu.VMEM((n, tokens, D), bf),
+            pltpu.VMEM((n, tokens, D), bf),
+            pltpu.VMEM((4 * far, size, D), bf),
+            pltpu.VMEM((4 * far, size, D), bf),
+            pltpu.SemaphoreType.DMA((2, 4 * far)),
+            pltpu.SemaphoreType.DMA((2, 4 * (far + 1))),
+            pltpu.SemaphoreType.DMA((2, 2 * far)),
+            pltpu.SemaphoreType.DMA((2, 4 * far)),
+            pltpu.SemaphoreType.DMA((4,)),
+        ],
+        compiler_params=pltpu.CompilerParams(
+            collective_id=1, has_side_effects=True, vmem_limit_bytes=VMEM_MOST
+        ),
+    )(packed, w_gate, w_up, w_down)
+
+
+def on_device_rings(
+    hidden_in, query_in, key_in, value_in, positions, segments, expert_ids,
+    w_out, w_router, w_gate, w_up, w_down, ring=0,
+):
+    tokens = hidden_in.shape[1]
+    angles = rope_angles(positions[:, 0, :])
+    query_rot = prepare(query_in[0], HEADS, angles)
+    key_rot = prepare(key_in[0], KV_HEADS, angles)
+    seg_cols = jnp.broadcast_to(segments[0].astype(jnp.bfloat16)[:, None], (tokens, META))
+    kv_rows = jnp.concatenate([key_rot, value_in[0], seg_cols], axis=1)
+    residual = attend_project(ring, query_rot, kv_rows, w_out, hidden_in[0])
+    normed = row_norm(residual.astype(jnp.float32)).astype(jnp.bfloat16)
+    logits = jnp.dot(normed, w_router, preferred_element_type=jnp.float32)
+    expert_count = w_router.shape[1]
+    own_ids = expert_ids[0]
+    expert_range = jnp.arange(expert_count, dtype=jnp.int32)
+    chosen = jnp.any(own_ids[:, :, None] == expert_range[None, None, :], axis=1)
+    raised = jnp.where(chosen, jnp.exp(logits), 0.0)
+    gates = raised / jnp.sum(raised, axis=-1, keepdims=True)
+    high = gates.astype(jnp.bfloat16)
+    low = (gates - high.astype(jnp.float32)).astype(jnp.bfloat16)
+    pad = jnp.zeros((tokens, META - 2 * expert_count), jnp.bfloat16)
+    packed = jnp.concatenate([normed, high, low, pad], axis=1)
+    capacity = 9 * tokens * TOP // (8 * expert_count)
+    mixture = expert_layer(ring, -(-capacity // 16) * 16, packed, w_gate, w_up, w_down)
+    layer_out = (residual.astype(jnp.float32) + mixture).astype(jnp.bfloat16)
+    return (residual[None], layer_out[None])
 
 
 def on_device(
@@ -217,8 +714,10 @@
         P(("ctx", "grp"), None, None),
         P(("ctx", "grp"), None, None),
     )
+    ring = mesh.shape["ctx"]
+    in_vmem = ring % 2 == 0 and ring <= 8 and mesh.shape["grp"] == 2
     return jax.shard_map(
-        on_device,
+        functools.partial(on_device_rings, ring=ring) if in_vmem else on_device,
         mesh=mesh,
         in_specs=placed,
         out_specs=(P(("parts", "grp"), "ctx", None), P(("parts", "grp"), "ctx", None)),

time: 339 us -> 193 us (0.57)
  Pallas kernels: 0 us -> 179 us
  waiting for transfers between devices: 158 us -> 0 us
  blocking collectives: 104 us -> 0 us
  matrix products: 40.3 us -> 0.36 us
  between operations: 14.7 us -> 0.99 us
  local copies, waits for them, and re-layouts: 8.65 us -> 3.38 us
  other arithmetic: 11.2 us -> 6.36 us
    pallas_call x0 -> x2, Pallas kernels: none -> 179 us  [the longest x1 119 us: expert_layer(): pl.pallas_call(functools.partial(expert_kernel, n, cap), out_shape=jax.Sh...]
    all_gather x4 -> x0, blocking collectives: 104 us -> none  [the longest x1 36.2 us: on_device(): lax.all_gather(chosen.astype(jnp.bfloat16), places, axis=0, tiled=False)]
    reduce_scatter x1 -> x0, waiting for transfers between devices: 103 us -> none  [on_device(): lax.psum_scatter(spread.reshape(blocks * tokens, D), places, scatter_dime...]
    all_gather x2 -> x0, waiting for transfers between devices: 54.9 us -> none  [the longest x1 54.7 us: on_device(): all_rows = lax.all_gather(normed, places, axis=0, tiled=False)]
    dot_general x10 -> x1, matrix products: 40.3 us -> 0.36 us  [on_device_rings(): logits = jnp.dot(normed, w_router, preferred_element_type=jnp.float32)]
  transfers between devices with their start and end apart: 3 -> 0, of which waited for: 3 -> 0; matrix products, arithmetic and copies ran while one was open for 6% -> 0% of each run, Pallas kernels for 0% -> 0%
where the time goes in v2:
time: 193 us; the launch traced here: 190 us
  Pallas kernels  179 us (93%)
  other arithmetic  6.36 us (3%)
  local copies, waits for them, and re-layouts  3.38 us (2%)
    pallas_call x1, Pallas kernels, expert_layer(): pl.pallas_call(functools.partial(expert_kernel, n, cap), out_shape=jax.Sh...  119 us
    pallas_call x1, Pallas kernels, attend_project(): pl.pallas_call(functools.partial(attend_kernel, n), out_shape=jax.ShapeDt...  60.4 us

profile of v2, /device:TPU:15, one launch (start us, length us, event | category | flops | bytes accessed | tf_op | source)
XLA Modules:
  0.0 190.4 jit_solution(10844902115661131288)
XLA Ops:
  0.6 1.2 convert_bitcast_fusion
  1.8 0.2 copy.50
  2.0 0.3 multiply_reduce_fusion
  2.5 0.1 copy.38
  2.6 0.3 broadcast_multiply_fusion
  3.0 0.6 gather_fusion
  3.6 0.2 cosine_bitcast_fusion
  4.0 0.5 subtract_convert_fusion
  4.5 0.3 pad_maximum_fusion
  4.8 0.1 copy.57
  5.1 0.2 multiply_reduce_fusion.1
  5.3 0.2 broadcast_multiply_fusion.1
  5.5 0.3 subtract_convert_fusion.1
  5.8 0.2 pad_maximum_fusion.2
  6.2 60.4 %shard_map.149 = bf16[128,2048]{1,0:T(8,128)(2,1)S(1)} custom-call(bf16[128,2048]{1,0:T(8,128)(2,1)S(1)} %bitcast.31, bf16[128,640]{1,0:T(8,128)(2,1)S(1)} %pad_maximum_fusion.1.kv_ref, bf16[128,2048]{1,0:T(8,128)(2,1)S(1)} %copy-done.1, bf16[128,2048]{1,0:T(8,128)(2,1)S(1)} %bitcast.32), custom_call_target="tpu_custom_call" | custom-call | tf_op jit(solution)/shard_map/pallas_call | solution.py:287
  66.6 0.2 fusion.1
  66.8 0.2 fusion.2
  67.0 0.1 copy.46
  67.1 0.4 fusion.7
  67.4 0.1 subtract_convert_fusion.2
  67.6 1.0 concatenate.17.x_ref
  68.5 118.9 %shard_map.150 = f32[128,2048]{1,0:T(8,128)} custom-call(bf16[128,2176]{1,0:T(8,128)(2,1)} %concatenate.17.x_ref, bf16[1,2048,768]{2,1,0:T(8,128)(2,1)} %wg_hbm.1, bf16[1,2048,768]{2,1,0:T(8,128)(2,1)} %wu_hbm.1, bf16[1,768,2048]{2,1,0:T(8,128)(2,1)} %wd_hbm.1), custom_call_target="tpu_custom_call" | custom-call | tf_op jit(solution)/shard_map/pallas_call | solution.py:534
  187.5 2.1 %fusion.4 = bf16[1,128,2048]{2,1,0:T(8,128)(2,1)} fusion(f32[128,2048]{1,0:T(8,128)} %shard_map.150, bf16[128,2048]{1,0:T(8,128)(2,1)S(1)} %shard_map.149), kind=kLoop, calls=%fused_computation.13 | loop fusion | flops 786432 | bytes 2097152 | tf_op jit(solution)/shard_map/broadcast_in_dim | solution.py:592
  189.6 0.8 copy.62
  (34 shorter events, 0.5 us)
Async XLA Ops:
  0.6 66.5 %copy-start = (bf16[2048,16]{0,1:T(8,128)(2,1)S(1)}, bf16[2048,16]{0,1:T(8,128)(2,1)}, u32[]{:S(2)}) copy-start(bf16[2048,16]{0,1:T(8,128)(2,1)} %param.22) | copy-start | bytes 196612
  1.8 1.1 copy-start.7
  1.8 1.1 copy-start.6
  3.6 1.4 copy-start.3
  4.0 2.0 %copy-start.8 = (s32[1,128]{1,0:T(1,128)S(1)}, s32[1,128]{1,0:T(1,128)}, u32[]{:S(2)}) copy-start(s32[1,128]{1,0:T(1,128)} %param.19) | copy-start | bytes 1540
  4.0 2.1 %copy-start.4 = (bf16[1,128,256]{2,1,0:T(8,128)(2,1)S(1)}, bf16[1,128,256]{2,1,0:T(8,128)(2,1)}, u32[]{:S(2)}) copy-start(bf16[1,128,256]{2,1,0:T(8,128)(2,1)} %param.17) | copy-start | bytes 196612
  4.5 1.7 copy-start.1
  4.5 1.7 copy-start.2
  5.0 62.0 %copy-start.5 = (s32[1,128,8]{1,2,0:T(8,128)S(1)}, s32[1,128,8]{1,2,0:T(8,128)}, u32[]{:S(2)}) copy-start(s32[1,128,8]{1,2,0:T(8,128)} %param.20) | copy-start | bytes 12292

commit v3 on v2

--- a/solution.py
+++ b/solution.py
@@ -102,7 +102,6 @@
 MESH = pl.DeviceIdType.MESH
 VMEM_MOST = 64 * 1000 * 1024
 NT = (((1,), (1,)), ((), ()))
-TN = (((0,), (0,)), ((), ()))
 
 
 def ring_place(index, n):
@@ -134,7 +133,7 @@
     pl.semaphore_wait(barrier, len(wheres))
 
 
-def attend_kernel(n, q_ref, kv_ref, w_ref, hid_ref, res_ref, kv_all, w_all, att, kv_sem, w_sem, p_sem, own_sem):
+def attend_kernel(n, q_ref, kv_ref, w_ref, hid_ref, res_ref, kv_all, w_all, att, near, kv_sem, w_sem, p_sem, own_sem):
     ctx = lax.axis_index("ctx")
     grp = lax.axis_index("grp")
     place = ring_place(ctx, n)
@@ -242,39 +241,57 @@
     query_pos = lax.broadcasted_iota(jnp.int32, (tokens, keys), 0) + ctx * tokens
     allowed = (key_pos <= query_pos) & (seg_of_key == seg_of_query)
 
-    def attend_heads(first, last):
-        @pl.loop(first, last)
-        def _(head):
-            at = pl.ds(pl.multiple_of(head * HD, HD), HD)
-            k_at = pl.ds(pl.multiple_of((head // group) * HD, HD), HD)
-            v_at = pl.ds(pl.multiple_of(width + (head // group) * HD, HD), HD)
-            scores = lax.dot_general(
-                q_ref[:, at], kv_all[:, k_at], NT, preferred_element_type=jnp.float32
-            ) * (1.0 / math.sqrt(HD))
-            weights = jnp.where(allowed, jnp.exp(scores), 0.0)
-            total = jnp.sum(weights, axis=-1, keepdims=True)
-            weighted = jnp.dot(
-                weights.astype(jnp.bfloat16), kv_all[:, v_at], preferred_element_type=jnp.float32
-            )
-            att[:, at] = (weighted / total).astype(jnp.bfloat16)
+    def attend_head(head):
+        at = slice(head * HD, (head + 1) * HD)
+        first = (head // group) * HD
+        scores = lax.dot_general(
+            q_ref[:, at], kv_all[:, first : first + HD], NT, preferred_element_type=jnp.float32
+        ) * (1.0 / math.sqrt(HD))
+        weights = jnp.where(allowed, jnp.exp(scores), 0.0)
+        total = jnp.sum(weights, axis=-1, keepdims=True)
+        weighted = jnp.dot(
+            weights.astype(jnp.bfloat16),
+            kv_all[:, width + first : width + first + HD],
+            preferred_element_type=jnp.float32,
+        )
+        att[:, at] = (weighted / total).astype(jnp.bfloat16)
 
     rest = events[done:]
-    pieces = 4
-    for piece in range(pieces):
-        attend_heads(piece * HEADS // pieces, (piece + 1) * HEADS // pieces)
-        if rest:
+    for head in range(HEADS):
+        attend_head(head)
+        if (head + 1) % 4 == 0 and len(rest) > 2:
             w_step(*rest.pop(0))
-    for event in rest:
-        w_step(*event)
+    while len(rest) > 2:
+        w_step(*rest.pop(0))
     own_w.wait()
     for copy in passed:
         copy.wait_recv()
-    tile = 512
+    waited = len(passed)
+    tile = 1024
+    deep = 2 * rows
+
+    def project(chip, at):
+        span = pl.ds(pl.multiple_of(chip * deep, deep), deep)
+        return jnp.dot(att[:, span], w_all[span, at], preferred_element_type=jnp.float32)
 
     @pl.loop(0, res_ref.shape[1] // tile)
     def _(index):
         at = pl.ds(pl.multiple_of(index * tile, tile), tile)
-        projected = jnp.dot(att[...], w_all[:, at], preferred_element_type=jnp.float32)
+        projected = project(ctx, at)
+        for hop in range(1, far):
+            for side in range(2):
+                projected = projected + project(source(side, hop), at)
+        near[:, at] = projected
+
+    for event in rest:
+        w_step(*event)
+    for copy in passed[waited:]:
+        copy.wait_recv()
+
+    @pl.loop(0, res_ref.shape[1] // tile)
+    def _(index):
+        at = pl.ds(pl.multiple_of(index * tile, tile), tile)
+        projected = near[:, at] + project(source(0, far), at)
         res_ref[:, at] = (hid_ref[:, at].astype(jnp.float32) + projected).astype(jnp.bfloat16)
 
     for copy in started + passed:
@@ -293,6 +310,7 @@
             pltpu.VMEM((keys, kv_rows.shape[1]), jnp.bfloat16),
             pltpu.VMEM((2 * n * w_out.shape[0], w_out.shape[1]), jnp.bfloat16),
             pltpu.VMEM(query_rot.shape, jnp.bfloat16),
+            pltpu.VMEM(hidden.shape, jnp.float32),
             pltpu.SemaphoreType.DMA((2, 4 * far)),
             pltpu.SemaphoreType.DMA((2, 4 * far)),
             pltpu.SemaphoreType.DMA((2, 4 * (far + 1))),
@@ -305,8 +323,8 @@
 
 
 def expert_kernel(
-    n, cap, x_ref, wg_hbm, wu_hbm, wd_hbm, out_ref,
-    x_all, wg, wu, wd, picks, rows_in, acts, scaled, gate_of, mine, other, theirs,
+    n, cap, x_ref, res_ref, wg_hbm, wu_hbm, wd_hbm, out_ref,
+    x_all, wg, wu, wd, picks, places, rows_in, acts, gate_of, contrib, theirs,
     r_out, r_in, a_sem, p_sem, s_sem, r_sem, l_sem,
 ):
     ctx = lax.axis_index("ctx")
@@ -340,8 +358,11 @@
         src = part_of(x_ref, part) if isinstance(hop, int) and hop == 0 else block
         return remote(src, block, p_sem, (side * 2 + part) * (far + 1) + hop, partner)
 
-    def s_copy(chip, slot):
-        return remote(other.at[chip], theirs.at[chip], s_sem, slot, partner)
+    def s_copy(side, hop):
+        chip = source(side, hop)
+        return remote(
+            contrib.at[chip * 2 + 1 - grp], theirs.at[chip], s_sem, side * (far + 1) + hop, partner
+        )
 
     for side in range(2):
         a_copy(side, side, 0).start()
@@ -367,49 +388,13 @@
         < lax.broadcasted_iota(jnp.int32, (tokens, tokens), 1)
     ).astype(jnp.bfloat16)
     slot_at = lax.broadcasted_iota(jnp.int32, (cap, tokens), 0)
-    tile = 256
-
-    @pl.loop(0, far)
-    def _(step):
-        hop = step + 1
-        for lead in (True, False):
-            for side in range(2):
-                part = side if lead else 1 - side
-
-                def take(side=side, part=part, lead=lead):
-                    a_copy(side, part, hop - 1).wait_recv()
-                    p_copy(side, part, hop).start()
-
-                    @pl.when(hop < hops(side, part))
-                    def _():
-                        a_copy(side, part, hop).start()
-
-                if lead:
-                    take()
-                else:
-                    pl.when(hop < far)(take)
-        p_copy(0, 0, hop).wait_recv()
-
-        @pl.when(hop < far)
-        def _():
-            p_copy(0, 1, hop).wait_recv()
-
-        @pl.when(hop == far)
-        def _():
-            p_copy(1, 1, far).wait_recv()
-
-        @pl.when(step == 0)
-        def _():
-            p_copy(0, 0, 0).wait_recv()
-            p_copy(0, 1, 0).wait_recv()
-
-        @pl.when(step > 0)
-        def _():
-            p_copy(1, 0, step).wait_recv()
-            p_copy(1, 1, step).wait_recv()
-
-        chips = [source(0, hop), source(1, step)]
-        for at in range(4):
+    ff_tile = math.gcd(wg.shape[1], 768)
+    tile = 1024
+
+    def hidden_units(chips):
+        count = 2 * len(chips)
+        rows = pl.ds(0, count * cap)
+        for at in range(count):
             block = chips[at // 2] * 2 + at % 2
             span = pl.ds(at * cap, cap)
             meta = x_all[block, :, width:]
@@ -424,58 +409,95 @@
             slot = jnp.where(chosen, rank, -1.0).astype(jnp.int32)[0:1]
             here = slot_at == slot
             picks[span] = here.astype(jnp.float32).astype(jnp.bfloat16)
+            places[at] = jnp.transpose(here.astype(jnp.float32)).astype(jnp.bfloat16)
             gate_of[span] = jnp.sum(jnp.where(here, gate_row, 0.0), axis=-1, keepdims=True)
 
-            @pl.loop(0, width // 512)
+            @pl.loop(0, width // 2048)
             def _(index):
-                cols = pl.ds(pl.multiple_of(index * 512, 512), 512)
+                cols = pl.ds(pl.multiple_of(index * 2048, 2048), 2048)
                 rows_in[span, cols] = jnp.dot(
                     picks[span], x_all[block, :, cols], preferred_element_type=jnp.float32
                 ).astype(jnp.bfloat16)
 
-        @pl.loop(0, wg.shape[1] // tile)
+        @pl.loop(0, wg.shape[1] // ff_tile)
         def _(index):
-            cols = pl.ds(pl.multiple_of(index * tile, tile), tile)
-            gate_part = jnp.dot(rows_in[...], wg[:, cols], preferred_element_type=jnp.float32)
-            up_part = jnp.dot(rows_in[...], wu[:, cols], preferred_element_type=jnp.float32)
+            cols = pl.ds(pl.multiple_of(index * ff_tile, ff_tile), ff_tile)
+            gate_part = jnp.dot(rows_in[rows], wg[:, cols], preferred_element_type=jnp.float32)
+            up_part = jnp.dot(rows_in[rows], wu[:, cols], preferred_element_type=jnp.float32)
             silu = gate_part / (1.0 + jnp.exp(-gate_part))
-            acts[:, cols] = (silu * up_part).astype(jnp.bfloat16)
+            acts[rows, cols] = (silu * up_part).astype(jnp.bfloat16)
+
+    def give_back(chips, copies):
+        count = 2 * len(chips)
+        rows = pl.ds(0, count * cap)
 
         @pl.loop(0, width // tile)
         def _(index):
             cols = pl.ds(pl.multiple_of(index * tile, tile), tile)
-            produced = jnp.dot(acts[...], wd[:, cols], preferred_element_type=jnp.float32)
-            weighted = (produced * gate_of[...]).astype(jnp.bfloat16)
-            for at in range(4):
-                spread = lax.dot_general(
-                    picks[at * cap : (at + 1) * cap],
+            produced = jnp.dot(acts[rows], wd[:, cols], preferred_element_type=jnp.float32)
+            weighted = (produced * gate_of[rows]).astype(jnp.bfloat16)
+            for at in range(count):
+                contrib[chips[at // 2] * 2 + at % 2, :, cols] = jnp.dot(
+                    places[at],
                     weighted[at * cap : (at + 1) * cap],
-                    TN,
                     preferred_element_type=jnp.float32,
                 ).astype(jnp.bfloat16)
-                scaled[at, :, cols] = spread
-
-        for at in range(2):
-            mine[chips[at]] = scaled[at * 2 + grp]
-            other[chips[at]] = scaled[at * 2 + 1 - grp]
-        for at in range(2):
-            s_copy(chips[at], at * far + step).start()
-
-    def taken(slot_side, step):
-        chip = source(0, step + 1) if slot_side == 0 else source(1, step)
-        s_copy(chip, slot_side * far + step).wait_recv()
+
+        for copy in copies:
+            copy.start()
+
+    def arrive(hop, lead, last=False):
+        for side in range(2):
+            part = side if lead else 1 - side
+            a_copy(side, part, hop - 1).wait_recv()
+            p_copy(side, part, hop).start()
+            if not last:
+
+                @pl.when(hop < hops(side, part))
+                def _():
+                    a_copy(side, part, hop).start()
+
+    def both(hop):
+        return [source(0, hop), source(1, hop)], [s_copy(0, hop), s_copy(1, hop)]
+
+    for part in range(2):
+        p_copy(0, part, 0).wait_recv()
+    hidden_units([ctx])
+    give_back([ctx], [s_copy(0, 0)])
+
+    @pl.loop(1, far)
+    def _(hop):
+        arrive(hop, True)
+
+        @pl.when(hop > 1)
+        def _():
+            give_back(*both(hop - 1))
+
+        arrive(hop, False)
+        for side in range(2):
+            for part in range(2):
+                p_copy(side, part, hop).wait_recv()
+        hidden_units(both(hop)[0])
+
+    give_back(*both(far - 1))
+    arrive(far, True, last=True)
+    for side in range(2):
+        p_copy(side, side, far).wait_recv()
+    hidden_units([source(0, far)])
+    give_back([source(0, far)], [s_copy(0, far)])
 
     def ready(place_off):
-        hop = place_off % n
-        if hop < far:
-            taken(1, hop)
+        away = place_off % n
+        if 0 < away < far:
+            s_copy(1, away).wait_recv()
         else:
-            taken(0, n - hop - 1)
+            s_copy(0, (n - away) % n).wait_recv()
 
     def pair_sum(place_off, part):
         chip = ring_index(place + place_off, n)
         span = pl.ds(part * size, size)
-        return mine[chip, span, :].astype(jnp.float32) + theirs[chip, span, :].astype(jnp.float32)
+        kept = contrib[chip * 2 + grp, span, :].astype(jnp.float32)
+        return kept + theirs[chip, span, :].astype(jnp.float32)
 
     def r_copy(side, part, hop):
         slot = (side * 2 + part) * far + hop
@@ -509,7 +531,8 @@
             last = hops(side, part) - 1
             r_copy(side, part, last).wait_recv()
             value = value + r_in[(side * 2 + part) * far + last].astype(jnp.float32)
-        out_ref[part * size : (part + 1) * size, :] = value
+        span = pl.ds(part * size, size)
+        out_ref[span, :] = (res_ref[span, :].astype(jnp.float32) + value).astype(jnp.bfloat16)
     for side in range(2):
         for part in range(2):
             for hop in range(hops(side, part)):
@@ -519,12 +542,13 @@
                 p_copy(side, part, hop).wait_send()
     for part in range(2):
         p_copy(0, part, 0).wait_send()
-    for step in range(far):
-        s_copy(source(0, step + 1), step).wait_send()
-        s_copy(source(1, step), far + step).wait_send()
-
-
-def expert_layer(n, cap, packed, w_gate, w_up, w_down):
+    for hop in range(far + 1):
+        s_copy(0, hop).wait_send()
+    for hop in range(1, far):
+        s_copy(1, hop).wait_send()
+
+
+def expert_layer(n, cap, packed, residual, w_gate, w_up, w_down):
     tokens, far = packed.shape[0], n // 2
     ff = w_gate.shape[2]
     vmem = pl.BlockSpec(memory_space=pltpu.VMEM)
@@ -533,8 +557,8 @@
     size = tokens // 2
     return pl.pallas_call(
         functools.partial(expert_kernel, n, cap),
-        out_shape=jax.ShapeDtypeStruct((tokens, D), jnp.float32),
-        in_specs=[vmem, hbm, hbm, hbm],
+        out_shape=jax.ShapeDtypeStruct((tokens, D), bf),
+        in_specs=[vmem, vmem, hbm, hbm, hbm],
         out_specs=vmem,
         scratch_shapes=[
             pltpu.VMEM((2 * n, tokens, packed.shape[1]), bf),
@@ -542,25 +566,24 @@
             pltpu.VMEM((D, ff), bf),
             pltpu.VMEM((ff, D), bf),
             pltpu.VMEM((4 * cap, tokens), bf),
+            pltpu.VMEM((4, tokens, cap), bf),
             pltpu.VMEM((4 * cap, D), bf),
             pltpu.VMEM((4 * cap, ff), bf),
-            pltpu.VMEM((4, tokens, D), bf),
             pltpu.VMEM((4 * cap, 1), jnp.float32),
-            pltpu.VMEM((n, tokens, D), bf),
-            pltpu.VMEM((n, tokens, D), bf),
+            pltpu.VMEM((2 * n, tokens, D), bf),
             pltpu.VMEM((n, tokens, D), bf),
             pltpu.VMEM((4 * far, size, D), bf),
             pltpu.VMEM((4 * far, size, D), bf),
             pltpu.SemaphoreType.DMA((2, 4 * far)),
             pltpu.SemaphoreType.DMA((2, 4 * (far + 1))),
-            pltpu.SemaphoreType.DMA((2, 2 * far)),
+            pltpu.SemaphoreType.DMA((2, 2 * (far + 1))),
             pltpu.SemaphoreType.DMA((2, 4 * far)),
             pltpu.SemaphoreType.DMA((4,)),
         ],
         compiler_params=pltpu.CompilerParams(
             collective_id=1, has_side_effects=True, vmem_limit_bytes=VMEM_MOST
         ),
-    )(packed, w_gate, w_up, w_down)
+    )(packed, residual, w_gate, w_up, w_down)
 
 
 def on_device_rings(
@@ -587,8 +610,8 @@
     pad = jnp.zeros((tokens, META - 2 * expert_count), jnp.bfloat16)
     packed = jnp.concatenate([normed, high, low, pad], axis=1)
     capacity = 9 * tokens * TOP // (8 * expert_count)
-    mixture = expert_layer(ring, -(-capacity // 16) * 16, packed, w_gate, w_up, w_down)
-    layer_out = (residual.astype(jnp.float32) + mixture).astype(jnp.bfloat16)
+    rows = -(-capacity // 16) * 16
+    layer_out = expert_layer(ring, rows, packed, residual, w_gate, w_up, w_down)
     return (residual[None], layer_out[None])
 
 

time: 193 us -> 173 us (0.90)
  Pallas kernels: 179 us -> 158 us
  local copies, waits for them, and re-layouts: 3.38 us -> 6.34 us
  other arithmetic: 6.36 us -> 4.3 us
    pallas_call x1, Pallas kernels: 119 us -> 99.1 us  [expert_layer(): pl.pallas_call(functools.partial(expert_kernel, n, cap), out_shape=jax.Sh...]
    unnamed x23 -> x26, local copies, waits for them, and re-layouts: 1.19 us -> 4.17 us
    broadcast_in_dim x1 -> x0, other arithmetic: 2.13 us -> none  [on_device_rings(): return (residual[None], layer_out[None])]
where the time goes in v3:
time: 173 us; the launch traced here: 170 us
  Pallas kernels  158 us (91%)
  local copies, waits for them, and re-layouts  6.34 us (4%)
  other arithmetic  4.3 us (2%)
    pallas_call x1, Pallas kernels, expert_layer(): pl.pallas_call(functools.partial(expert_kernel, n, cap), out_shape=jax.Sh...  99.1 us
    pallas_call x1, Pallas kernels, attend_project(): pl.pallas_call(functools.partial(attend_kernel, n), out_shape=jax.ShapeDt...  59 us
    unnamed x26, local copies, waits for them, and re-layouts  4.17 us

profile of v3, /device:TPU:15, one launch (start us, length us, event | category | flops | bytes accessed | tf_op | source)
XLA Modules:
  0.0 170.2 jit_solution(14048157345354941872)
XLA Ops:
  0.6 1.2 convert_bitcast_fusion
  1.8 0.2 copy.50
  2.0 0.3 multiply_reduce_fusion
  2.5 0.1 copy.38
  2.6 0.4 broadcast_multiply_fusion
  3.0 0.6 gather_fusion
  3.6 0.2 cosine_bitcast_fusion
  4.0 0.5 subtract_convert_fusion
  4.6 0.3 pad_maximum_fusion
  4.9 0.1 copy.57
  5.1 0.2 multiply_reduce_fusion.1
  5.4 0.2 broadcast_multiply_fusion.1
  5.6 0.3 subtract_convert_fusion.1
  5.9 0.2 pad_maximum_fusion.2
  6.2 59.0 %shard_map.149.res_ref = bf16[128,2048]{1,0:T(8,128)(2,1)S(1)} custom-call(bf16[128,2048]{1,0:T(8,128)(2,1)S(1)} %bitcast.30, bf16[128,640]{1,0:T(8,128)(2,1)S(1)} %pad_maximum_fusion.1.kv_ref, bf16[128,2048]{1,0:T(8,128)(2,1)S(1)} %copy-done.2, bf16[128,2048]{1,0:T(8,128)(2,1)S(1)} %bitcast.31), custom_call_target="tpu_custom_call" | custom-call | tf_op jit(solution)/shard_map/pallas_call | solution.py:304
  65.3 0.2 fusion.1
  65.5 0.2 fusion.2
  65.7 0.1 copy.46
  65.8 0.4 fusion.5
  66.2 0.1 subtract_convert_fusion.2
  66.3 1.0 concatenate.17.x_ref
  67.3 99.1 %shard_map.150 = bf16[128,2048]{1,0:T(8,128)(2,1)} custom-call(bf16[128,2176]{1,0:T(8,128)(2,1)} %concatenate.17.x_ref, bf16[128,2048]{1,0:T(8,128)(2,1)} %copy-done.1, bf16[1,2048,768]{2,1,0:T(8,128)(2,1)} %wg_hbm.1, bf16[1,2048,768]{2,1,0:T(8,128)(2,1)} %wu_hbm.1, bf16[1,768,2048]{2,1,0:T(8,128)(2,1)} %wd_hbm.1), custom_call_target="tpu_custom_call" | custom-call | tf_op jit(solution)/shard_map/pallas_call | solution.py:558
  166.4 1.9 %copy.63 = bf16[1,128,2048]{2,1,0:T(8,128)(2,1)} copy(bf16[1,128,2048]{2,1,0:T(8,128)(2,1)} %bitcast.29) | data formatting | bytes 1048576
  168.3 1.9 %copy.64 = bf16[1,128,2048]{2,1,0:T(8,128)(2,1)} copy(bf16[1,128,2048]{2,1,0:T(8,128)(2,1)} %bitcast.35) | data formatting | bytes 1048576
  (36 shorter events, 0.6 us)
Async XLA Ops:
  0.6 65.2 %copy-start = (bf16[2048,16]{0,1:T(8,128)(2,1)S(1)}, bf16[2048,16]{0,1:T(8,128)(2,1)}, u32[]{:S(2)}) copy-start(bf16[2048,16]{0,1:T(8,128)(2,1)} %param.22) | copy-start | bytes 196612
  1.8 1.1 copy-start.8
  1.8 1.1 copy-start.7
  3.6 1.5 copy-start.4
  4.0 2.1 %copy-start.9 = (s32[1,128]{1,0:T(1,128)S(1)}, s32[1,128]{1,0:T(1,128)}, u32[]{:S(2)}) copy-start(s32[1,128]{1,0:T(1,128)} %param.19) | copy-start | bytes 1540
  4.0 2.2 %copy-start.5 = (bf16[1,128,256]{2,1,0:T(8,128)(2,1)S(1)}, bf16[1,128,256]{2,1,0:T(8,128)(2,1)}, u32[]{:S(2)}) copy-start(bf16[1,128,256]{2,1,0:T(8,128)(2,1)} %param.17) | copy-start | bytes 196612
  4.6 1.7 copy-start.2
  4.6 1.7 copy-start.3
  5.0 60.6 %copy-start.6 = (s32[1,128,8]{1,2,0:T(8,128)S(1)}, s32[1,128,8]{1,2,0:T(8,128)}, u32[]{:S(2)}) copy-start(s32[1,128,8]{1,2,0:T(8,128)} %param.20) | copy-start | bytes 12292
  65.3 2.0 %copy-start.1 = (bf16[128,2048]{1,0:T(8,128)(2,1)}, bf16[128,2048]{1,0:T(8,128)(2,1)S(1)}, u32[]{:S(2)}) copy-start(bf16[128,2048]{1,0:T(8,128)(2,1)S(1)} %shard_map.149.res_ref) | copy-start | bytes 1572868
